TPU v7x, 32 devices: a whole 2x2x4 slice. The times are simulated.
32 devices in a mesh: dp: 16 (over z, y, x), mp: 2 (over core).
Axes of the slice: x: 2, y: 2, z: 4, core: 2. Of those that a mesh axis runs over, the one named last changes fastest.
Arguments:
- tokens: bfloat16 [32768, 768], P('dp'), may hold values from -6 to 6
- cond: bfloat16 [32768, 128], P('dp'), may hold values from -6 to 6
- segments: int32 [32, 1024], P('dp'), may hold values from 0 to 3, never falling along the last dimension, each value on 1 to 512 neighbouring positions
- out_grad: bfloat16 [32768, 768], P('dp'), may hold values from -6 to 6
- step: int32 [1], replicated, may hold values from 2 to 20
- ada_weight: float32 [128, 4608], P(None, 'dp'), may hold values from -0.5 to 0.5
- ada_first: float32 [128, 4608], P(None, 'dp'), may hold values from -0.00061035156 to 0.00061035156
- ada_second: float32 [128, 4608], P(None, 'dp'), may hold values from 1.3031258e-10 to 5.212503e-10
- norm_params: float32 [8, 768], P(None, 'dp'), may hold values from 0.5 to 1.5
- norm_first: float32 [8, 768], P(None, 'dp'), may hold values from -0.0024414062 to 0.0024414062
- norm_second: float32 [8, 768], P(None, 'dp'), may hold values from 2.6062516e-10 to 1.0425006e-09
- qkv_weight: float32 [3, 768, 768], P(None, 'dp', 'mp'), may hold values from -0.109375 to 0.109375
- qkv_first: float32 [3, 768, 768], P(None, 'dp', 'mp'), may hold values from -0.00061035156 to 0.00061035156
- qkv_second: float32 [3, 768, 768], P(None, 'dp', 'mp'), may hold values from 1.3031258e-10 to 5.212503e-10
- out_weight: float32 [768, 768], P('mp', 'dp'), may hold values from -1.75 to 1.75
- out_first: float32 [768, 768], P('mp', 'dp'), may hold values from -0.00061035156 to 0.00061035156
- out_second: float32 [768, 768], P('mp', 'dp'), may hold values from 1.6289073e-11 to 6.515629e-11
- up_weight: float32 [768, 3072], P('dp', 'mp'), may hold values from -0.21875 to 0.21875
- up_first: float32 [768, 3072], P('dp', 'mp'), may hold values from -0.00061035156 to 0.00061035156
- up_second: float32 [768, 3072], P('dp', 'mp'), may hold values from 1.3031258e-10 to 5.212503e-10
- down_weight: float32 [3072, 768], P('mp', 'dp'), may hold values from -0.109375 to 0.109375
- down_first: float32 [3072, 768], P('mp', 'dp'), may hold values from -0.00061035156 to 0.00061035156
- down_second: float32 [3072, 768], P('mp', 'dp'), may hold values from 1.3031258e-10 to 5.212503e-10
Outputs:
- result: bfloat16 [32768, 768], P('dp')
- input_grad: float32 [32768, 768], P('dp')
- grad_norm: float32 [1], replicated
- ada_weight_next: float32 [128, 4608], P(None, 'dp')
- ada_first_next: float32 [128, 4608], P(None, 'dp')
- ada_second_next: float32 [128, 4608], P(None, 'dp')
- norm_params_next: float32 [8, 768], P(None, 'dp')
- norm_first_next: float32 [8, 768], P(None, 'dp')
- norm_second_next: float32 [8, 768], P(None, 'dp')
- qkv_weight_next: float32 [3, 768, 768], P(None, 'dp', 'mp')
- qkv_first_next: float32 [3, 768, 768], P(None, 'dp', 'mp')
- qkv_second_next: float32 [3, 768, 768], P(None, 'dp', 'mp')
- out_weight_next: float32 [768, 768], P('mp', 'dp')
- out_first_next: float32 [768, 768], P('mp', 'dp')
- out_second_next: float32 [768, 768], P('mp', 'dp')
- up_weight_next: float32 [768, 3072], P('dp', 'mp')
- up_first_next: float32 [768, 3072], P('dp', 'mp')
- up_second_next: float32 [768, 3072], P('dp', 'mp')
- down_weight_next: float32 [3072, 768], P('mp', 'dp')
- down_first_next: float32 [3072, 768], P('mp', 'dp')
- down_second_next: float32 [3072, 768], P('mp', 'dp')
Inputs may be any that keep to these rules, and one draw needn't show every extreme that they name: `segments`: along each sequence document ids never fall; each document holds 1 to 512 positions, and one document of a sequence holds exactly 512.
All inputs are finite; a program needn't handle non-finite values.
Results may differ from a plain program's by a relative error of at most 0.012.
The roundings to bfloat16 on the way count: a program that leaves them out, or rounds other values in their place, can miss the bound.
Values may be sent and summed in bfloat16 or wider, within the bound.
A program may use at most 320 MiB of HBM per device.

v0:
```python
import math
import jax
import jax.numpy as jnp
from jax import lax
from jax.sharding import PartitionSpec as P

HEAD_DIM = 64
clip_limit = 1.0
step_rates = (0.075, 0.75, 0.075, 0.25, 0.075, 0.075)
decay_rates = (0.01, 0.0, 0.01, 0.01, 0.01, 0.01)


def modnorm(inputs, gain_row, shift_row, scale_row):
    centre = inputs - jnp.mean(inputs, axis=-1, keepdims=True)
    spread = jnp.mean(centre * centre, axis=-1, keepdims=True)
    return centre * lax.rsqrt(spread + 1e-05) * gain_row * (1.0 + scale_row) + shift_row


def rope_tables(length, head_size):
    half_dim = head_size // 2
    inverse = jnp.exp(
        jnp.arange(half_dim, dtype=jnp.float32) * (-2.0 * math.log(10000.0) / head_size)
    )
    angles = jnp.arange(length, dtype=jnp.float32)[:, None] * inverse[None, :]
    return (jnp.cos(angles), jnp.sin(angles))


def rotate(values, cosines, sines):
    half_dim = values.shape[-1] // 2
    first_half = values[..., :half_dim]
    second_half = values[..., half_dim:]
    cos_row = cosines[:, None, :]
    sin_row = sines[:, None, :]
    return jnp.concatenate(
        [
            first_half * cos_row - second_half * sin_row,
            second_half * cos_row + first_half * sin_row,
        ],
        axis=-1,
    )


def unrotate(grads, cosines, sines):
    half_dim = grads.shape[-1] // 2
    first_half = grads[..., :half_dim]
    second_half = grads[..., half_dim:]
    cos_row = cosines[:, None, :]
    sin_row = sines[:, None, :]
    return jnp.concatenate(
        [
            first_half * cos_row + second_half * sin_row,
            second_half * cos_row - first_half * sin_row,
        ],
        axis=-1,
    )


def gelu_tanh(values):
    return jax.nn.gelu(values, approximate=True)


def adam_update(
    weight, first_moment, second_moment, grad_mean, clip_factor, step_count, step_rate, decay_rate
):
    clipped = grad_mean * clip_factor
    first_new = 0.9 * first_moment + 0.1 * clipped
    second_new = 0.999 * second_moment + 0.001 * clipped * clipped
    fix_one = 1.0 - jnp.exp(step_count * math.log(0.9))
    fix_two = 1.0 - jnp.exp(step_count * math.log(0.999))
    update = first_new / fix_one / (jnp.sqrt(second_new / fix_two) + 1e-08) + decay_rate * weight
    return (weight - step_rate * update, first_new, second_new)


def per_device(
    tokens,
    cond,
    segments,
    out_grad,
    step,
    ada_weight,
    ada_first,
    ada_second,
    norm_params,
    norm_first,
    norm_second,
    qkv_weight,
    qkv_first,
    qkv_second,
    out_weight,
    out_first,
    out_second,
    up_weight,
    up_first,
    up_second,
    down_weight,
    down_first,
    down_second,
):
    ada_low, norm_low, qkv_low, out_low, up_low, down_low = (
        lax.all_gather(ada_weight.astype(jnp.bfloat16), "dp", axis=1, tiled=True),
        lax.all_gather(norm_params.astype(jnp.bfloat16), "dp", axis=1, tiled=True),
        lax.all_gather(qkv_weight.astype(jnp.bfloat16), "dp", axis=1, tiled=True),
        lax.all_gather(out_weight.astype(jnp.bfloat16), "dp", axis=1, tiled=True),
        lax.all_gather(up_weight.astype(jnp.bfloat16), "dp", axis=0, tiled=True),
        lax.all_gather(down_weight.astype(jnp.bfloat16), "dp", axis=1, tiled=True),
    )
    model_width = norm_low.shape[1]
    tok_rows = tokens.shape[0]
    seq_count = segments.shape[0]
    seq_length = segments.shape[1]
    heads_local = qkv_low.shape[2] // HEAD_DIM
    score_scale = HEAD_DIM ** (-0.5)
    cosines, sines = rope_tables(seq_length, HEAD_DIM)
    inputs = tokens.astype(jnp.float32)
    cond_low = jax.nn.silu(cond.astype(jnp.float32)).astype(jnp.bfloat16)
    norm_vals = norm_low.astype(jnp.float32)
    modulation = jnp.dot(cond_low, ada_low, preferred_element_type=jnp.float32) + norm_vals[
        2:
    ].reshape(-1)
    shift_one = modulation[:, 0:model_width]
    scale_one = modulation[:, model_width : 2 * model_width]
    gate_one = modulation[:, 2 * model_width : 3 * model_width]
    shift_two = modulation[:, 3 * model_width : 4 * model_width]
    scale_two = modulation[:, 4 * model_width : 5 * model_width]
    gate_two = modulation[:, 5 * model_width : 6 * model_width]
    h_one = modnorm(inputs, norm_vals[0], shift_one, scale_one).astype(jnp.bfloat16)
    projected = jnp.einsum("td,cde->cte", h_one, qkv_low, preferred_element_type=jnp.float32)
    shaped = projected.reshape(3, seq_count, seq_length, heads_local, HEAD_DIM)
    queries = rotate(shaped[0], cosines, sines).astype(jnp.bfloat16)
    keys = rotate(shaped[1], cosines, sines).astype(jnp.bfloat16)
    values = shaped[2].astype(jnp.bfloat16)

    def scores_of(query_block, key_block, segment_row):
        raw_scores = jnp.einsum(
            "qhd,khd->hqk", query_block, key_block, preferred_element_type=jnp.float32
        )
        same_doc = segment_row[:, None] == segment_row[None, :]
        return jnp.where(same_doc[None], raw_scores * score_scale, -1e30)

    def attend(packed):
        query_block, key_block, value_block, segment_row = packed
        scores = scores_of(query_block, key_block, segment_row)
        row_top = jnp.max(scores, axis=-1, keepdims=True)
        row_total = jnp.sum(jnp.exp(scores - row_top), axis=-1, keepdims=True)
        logsum = row_top + jnp.log(row_total)
        softmax_w = jnp.exp(scores - logsum).astype(jnp.bfloat16)
        mixed_out = jnp.einsum(
            "hqk,khd->qhd", softmax_w, value_block, preferred_element_type=jnp.float32
        )
        return (mixed_out.astype(jnp.bfloat16), logsum)

    attended, logsums = lax.map(attend, (queries, keys, values, segments))
    attn_flat = attended.reshape(tok_rows, -1)
    attn_part = jnp.dot(attn_flat, out_low, preferred_element_type=jnp.float32)
    branch = lax.psum(attn_part, "mp")
    middle = inputs + gate_one * branch
    h_two = modnorm(middle, norm_vals[1], shift_two, scale_two).astype(jnp.bfloat16)
    hidden_pre = jnp.dot(h_two, up_low, preferred_element_type=jnp.float32)
    hidden = gelu_tanh(hidden_pre).astype(jnp.bfloat16)
    mlp_part = jnp.dot(hidden, down_low, preferred_element_type=jnp.float32)
    cotangent = out_grad.astype(jnp.float32)
    mlp_out = lax.psum(mlp_part, "mp")
    result = (middle + gate_two * mlp_out).astype(jnp.bfloat16)
    d_gate_two = cotangent * mlp_out
    mlp_grad = (gate_two * cotangent).astype(jnp.bfloat16)
    grad_down = jnp.einsum("tf,td->fd", hidden, mlp_grad, preferred_element_type=jnp.float32)
    grad_hidden = jnp.einsum("td,fd->tf", mlp_grad, down_low, preferred_element_type=jnp.float32)
    unused_gelu, gelu_back = jax.vjp(gelu_tanh, hidden_pre)
    grad_pre = gelu_back(grad_hidden)[0].astype(jnp.bfloat16)
    grad_up = jnp.einsum("td,tf->df", h_two, grad_pre, preferred_element_type=jnp.float32)
    h_two_part = jnp.einsum("tf,df->td", grad_pre, up_low, preferred_element_type=jnp.float32)
    h_two_grad = lax.psum(h_two_part, "mp")
    unused_two, norm_two_back = jax.vjp(modnorm, middle, norm_vals[1], shift_two, scale_two)
    d_middle, d_gain_two, d_shift_two, d_scale_two = norm_two_back(h_two_grad)
    middle_grad = cotangent + d_middle
    attn_grad = (gate_one * middle_grad).astype(jnp.bfloat16)
    d_gate_one = middle_grad * branch
    grad_out = jnp.einsum("te,td->ed", attn_flat, attn_grad, preferred_element_type=jnp.float32)
    out_back = jnp.einsum(
        "td,ed->te", attn_grad, out_low, preferred_element_type=jnp.float32
    ).astype(jnp.bfloat16)
    grad_attended = out_back.reshape(seq_count, seq_length, heads_local, HEAD_DIM)

    def attend_back(packed):
        query_block, key_block, value_block, segment_row, logsum, upstream = packed
        scores = scores_of(query_block, key_block, segment_row)
        softmax_w = jnp.exp(scores - logsum)
        grad_weights = jnp.einsum(
            "qhd,khd->hqk", upstream, value_block, preferred_element_type=jnp.float32
        )
        grad_value = jnp.einsum(
            "hqk,qhd->khd",
            softmax_w.astype(jnp.bfloat16),
            upstream,
            preferred_element_type=jnp.float32,
        )
        row_delta = jnp.sum(softmax_w * grad_weights, axis=-1, keepdims=True)
        grad_scores = (softmax_w * (grad_weights - row_delta) * score_scale).astype(jnp.bfloat16)
        grad_query = jnp.einsum(
            "hqk,khd->qhd", grad_scores, key_block, preferred_element_type=jnp.float32
        )
        grad_key = jnp.einsum(
            "hqk,qhd->khd", grad_scores, query_block, preferred_element_type=jnp.float32
        )
        return (grad_query, grad_key, grad_value)

    grad_q, grad_k, grad_v = lax.map(
        attend_back, (queries, keys, values, segments, logsums, grad_attended)
    )
    grad_proj = (
        jnp.stack([unrotate(grad_q, cosines, sines), unrotate(grad_k, cosines, sines), grad_v])
        .reshape(3, tok_rows, -1)
        .astype(jnp.bfloat16)
    )
    grad_qkv = jnp.einsum("td,cte->cde", h_one, grad_proj, preferred_element_type=jnp.float32)
    h_one_part = jnp.einsum("cte,cde->td", grad_proj, qkv_low, preferred_element_type=jnp.float32)
    h_one_grad = lax.psum(h_one_part, "mp")
    unused_one, norm_one_back = jax.vjp(modnorm, inputs, norm_vals[0], shift_one, scale_one)
    d_inputs, d_gain_one, d_shift_one, d_scale_one = norm_one_back(h_one_grad)
    input_grad = middle_grad + d_inputs
    grad_mod = jnp.concatenate(
        [d_shift_one, d_scale_one, d_gate_one, d_shift_two, d_scale_two, d_gate_two], axis=1
    ).astype(jnp.bfloat16)
    grad_ada = jnp.einsum("tc,tm->cm", cond_low, grad_mod, preferred_element_type=jnp.float32)
    bias_grad = jnp.sum(grad_mod.astype(jnp.float32), axis=0).reshape(6, model_width)
    grad_norm_rows = jnp.concatenate([d_gain_one[None], d_gain_two[None], bias_grad], axis=0)
    ada_sum, norm_sum, qkv_sum, out_sum, up_sum, down_sum = (
        lax.psum_scatter(grad_ada, "dp", scatter_dimension=1, tiled=True),
        lax.psum_scatter(grad_norm_rows, "dp", scatter_dimension=1, tiled=True),
        lax.psum_scatter(grad_qkv, "dp", scatter_dimension=1, tiled=True),
        lax.psum_scatter(grad_out, "dp", scatter_dimension=1, tiled=True),
        lax.psum_scatter(grad_up, "dp", scatter_dimension=0, tiled=True),
        lax.psum_scatter(grad_down, "dp", scatter_dimension=1, tiled=True),
    )
    token_total = float(tok_rows * lax.axis_size("dp"))
    ada_mean = ada_sum / token_total
    norm_mean = norm_sum / token_total
    qkv_mean = qkv_sum / token_total
    out_mean = out_sum / token_total
    up_mean = up_sum / token_total
    down_mean = down_sum / token_total
    shared_part = 1.0 / lax.axis_size("mp")
    local_sq = (
        jnp.sum(qkv_mean * qkv_mean)
        + jnp.sum(out_mean * out_mean)
        + jnp.sum(up_mean * up_mean)
        + jnp.sum(down_mean * down_mean)
        + shared_part * (jnp.sum(ada_mean * ada_mean) + jnp.sum(norm_mean * norm_mean))
    )
    total_sq = lax.psum(local_sq, ("dp", "mp"))
    grad_norm = jnp.sqrt(total_sq)
    clip_factor = jnp.minimum(1.0, clip_limit / (grad_norm + 1e-06))
    step_count = step[0].astype(jnp.float32)
    ada_new = adam_update(
        ada_weight,
        ada_first,
        ada_second,
        ada_mean,
        clip_factor,
        step_count,
        step_rates[0],
        decay_rates[0],
    )
    norm_new = adam_update(
        norm_params,
        norm_first,
        norm_second,
        norm_mean,
        clip_factor,
        step_count,
        step_rates[1],
        decay_rates[1],
    )
    qkv_new = adam_update(
        qkv_weight,
        qkv_first,
        qkv_second,
        qkv_mean,
        clip_factor,
        step_count,
        step_rates[2],
        decay_rates[2],
    )
    out_new = adam_update(
        out_weight,
        out_first,
        out_second,
        out_mean,
        clip_factor,
        step_count,
        step_rates[3],
        decay_rates[3],
    )
    up_new = adam_update(
        up_weight,
        up_first,
        up_second,
        up_mean,
        clip_factor,
        step_count,
        step_rates[4],
        decay_rates[4],
    )
    down_new = adam_update(
        down_weight,
        down_first,
        down_second,
        down_mean,
        clip_factor,
        step_count,
        step_rates[5],
        decay_rates[5],
    )
    return (
        result,
        input_grad,
        grad_norm.reshape(1),
        ada_new[0],
        ada_new[1],
        ada_new[2],
        norm_new[0],
        norm_new[1],
        norm_new[2],
        qkv_new[0],
        qkv_new[1],
        qkv_new[2],
        out_new[0],
        out_new[1],
        out_new[2],
        up_new[0],
        up_new[1],
        up_new[2],
        down_new[0],
        down_new[1],
        down_new[2],
    )


def solution(mesh):
    return jax.shard_map(
        per_device,
        mesh=mesh,
        in_specs=(
            P("dp", None),
            P("dp", None),
            P("dp", None),
            P("dp", None),
            P(),
            P(None, "dp"),
            P(None, "dp"),
            P(None, "dp"),
            P(None, "dp"),
            P(None, "dp"),
            P(None, "dp"),
            P(None, "dp", "mp"),
            P(None, "dp", "mp"),
            P(None, "dp", "mp"),
            P("mp", "dp"),
            P("mp", "dp"),
            P("mp", "dp"),
            P("dp", "mp"),
            P("dp", "mp"),
            P("dp", "mp"),
            P("mp", "dp"),
            P("mp", "dp"),
            P("mp", "dp"),
        ),
        out_specs=(
            P("dp", None),
            P("dp", None),
            P(),
            P(None, "dp"),
            P(None, "dp"),
            P(None, "dp"),
            P(None, "dp"),
            P(None, "dp"),
            P(None, "dp"),
            P(None, "dp", "mp"),
            P(None, "dp", "mp"),
            P(None, "dp", "mp"),
            P("mp", "dp"),
            P("mp", "dp"),
            P("mp", "dp"),
            P("dp", "mp"),
            P("dp", "mp"),
            P("dp", "mp"),
            P("mp", "dp"),
            P("mp", "dp"),
            P("mp", "dp"),
        ),
        check_vma=False,
    )
```

profile of v0, /device:TPU:0, one launch (start us, length us, event | category | flops | bytes accessed | tf_op | source)
XLA Modules:
  0.0 1853.0 jit_solution(10040764894950794897)
XLA Ops:
  16.6 42.8 %all-gather = bf16[16,48,8]{1,2,0:T(8,128)(2,1)S(1)} all-gather(bf16[1,48,8]{1,2,0:T(8,128)(2,1)S(1)} %convert_bitcast_fusion), channel_id=1, replica_groups=mesh['dp'=16,'mp'=2] {'dp'}, dimensions={0}, use_global_device_ids=true | all-gather | bytes 13056 | tf_op jit(solution)/shard_map/all_gather | solution.py:101
  60.7 43.1 %all_gather.21 = bf16[384,768]{0,1:T(8,128)(2,1)} all-gather(bf16[384,48]{0,1:T(8,128)(2,1)S(1)} %convert_element_type.96), channel_id=1, replica_groups=mesh['dp'=16,'mp'=2] {'dp'}, dimensions={1}, use_global_device_ids=true | all-gather | bytes 626688 | tf_op jit(solution)/shard_map/all_gather | solution.py:103
  103.8 16.4 convolution_add_fusion
  174.8 70.6 %while.26 = (s32[]{:T(128)}, bf16[2,1024,6,64]{1,3,2,0:T(8,128)(2,1)S(1)}, f32[2,6,1024,1]{2,1,3,0:T(8,128)S(1)}, bf16[2,1024,6,64]{1,3,2,0:T(8,128)(2,1)}, s32[...) while((s32[]{:T(128)}, ...), condition=%wide.region_5.6_spmd, body=%wide.region_2.5_spmd.sunk | while | flops 1681254400 | bytes 83089512 | solution.py:152
  255.9 28.3 %all-reduce.7.cloned.1.call-done = f32[2048,768]{1,0:T(8,128)} async-done(((f32[2048,768]{1,0:T(8,128)}), f32[2048,768]{1,0:T(8,128)}) %all-reduce.7.cloned.1.call-update) | async-done | bytes 6291472 | tf_op jit(solution)/shard_map/psum | solution.py:155
  299.2 52.1 %all-gather.10.cloned.1.call-done = bf16[768,1536]{1,0:T(8,128)(2,1)} async-done(((bf16[48,1536]{1,0:T(8,128)(2,1)}), bf16[768,1536]{1,0:T(8,128)(2,1)}) %all-gather.10.cloned.1.call-update) | async-done | bytes 2359312 | tf_op jit(solution)/shard_map/all_gather | solution.py:104
  364.3 51.7 %all-gather.12.cloned.1.call-done = bf16[1536,768]{0,1:T(8,128)(2,1)} async-done(((bf16[1536,48]{0,1:T(8,128)(2,1)}), bf16[1536,768]{0,1:T(8,128)(2,1)}) %all-gather.12.cloned.1.call-update) | async-done | bytes 2359312 | tf_op jit(solution)/shard_map/all_gather | solution.py:105
  451.9 20.8 %all-reduce.9.cloned.1.call-done = f32[2048,768]{1,0:T(8,128)} async-done(((f32[2048,768]{1,0:T(8,128)}), f32[2048,768]{1,0:T(8,128)}) %all-reduce.9.cloned.1.call-update) | async-done | bytes 6291472 | tf_op jit(solution)/shard_map/psum | solution.py:172
  500.0 338.8 %while.27 = (s32[]{:T(128)}, f32[2,1024,6,64]{1,0,3,2:T(2,128)}, f32[2,1024,6,64]{1,0,3,2:T(2,128)}, bf16[2,1024,6,64]{1,3,2,0:T(8,128)(2,1)}, bf16[2,1024,6,64]...) while((s32[]{:T(128)}, f32[2,1024,6,64]{1,0,3,2:T(2,128)}, ...), condition=%wide.region_15.16_spmd, body=%wide.region_13.15_spmd.sunk | while | flops 4191172608 | bytes 306142336 | solution.py:207
  539.6 35.6 %fusion.212 = f32[1,1024,6,64]{1,3,2,0:T(8,128)} fusion(f32[6,1024,1024]{1,2,0:T(8,128)} %fusion.209, f32[6,1024,1024]{1,2,0:T(8,128)} %fusion.210, f32[6,1024]{1,0:T(8,128)S(1)} %dynamic-slice_bitcast_fusion.2, pred[1024,1024]{0,1:T(8,128)(4,1)S(1)} %broadcast_compare_fusion.5, bf16[2,1024,6,64]{1,3,2,0:T(8,128)(2,1)} %get-tuple-element.508, ...), kind=kOutput, calls=%fused_computation.45.clone.1 | convolution fusion | flops 874519552 | bytes 105185280 | tf_op jit(solution)/shard_map/while/body/eval_jaxpr/hqk,qhd->khd/dot_general | solution.py:202
  575.2 34.4 %fusion.211 = f32[1,1024,6,64]{1,3,2,0:T(8,128)S(1)} fusion(f32[6,1024,1024]{1,2,0:T(8,128)} %fusion.209, f32[6,1024,1024]{1,2,0:T(8,128)} %fusion.210, f32[6,1024]{1,0:T(8,128)S(1)} %dynamic-slice_bitcast_fusion.2, pred[1024,1024]{0,1:T(8,128)(4,1)S(1)} %broadcast_compare_fusion.5, bf16[2,1024,6,64]{1,3,2,0:T(8,128)(2,1)} %get-tuple-element.506, ...), kind=kOutput, calls=%fused_computation.44.clone.1 | convolution fusion | flops 874519552 | bytes 105185280 | tf_op jit(solution)/shard_map/while/body/eval_jaxpr/hqk,khd->qhd/dot_general | solution.py:199
  614.4 27.5 %dynamic_update_slice.30 = f32[2,1024,6,64]{1,0,3,2:T(2,128)} dynamic-update-slice(f32[2,1024,6,64]{1,0,3,2:T(2,128)} %get-tuple-element.492, f32[1,1024,6,64]{1,0,3,2:T(1,128)S(1)} %copy.200, s32[]{:T(128)S(6)} %copy.221, s32[]{:T(128)} %constant.54.clone.1..sunk, s32[]{:T(128)} %constant.54.clone.1..sunk, s32[]{:T(128)} %constant.54.clone.1..sunk) | dynamic-update-slice | bytes 3145732 | tf_op jit(solution)/shard_map/while/body/jit(dynamic_update_index_in_dim)/dynamic_update_slice | solution.py:207
  641.9 27.5 %dynamic_update_slice.29 = f32[2,1024,6,64]{1,0,3,2:T(2,128)} dynamic-update-slice(f32[2,1024,6,64]{1,0,3,2:T(2,128)} %get-tuple-element.491, f32[1,1024,6,64]{1,0,3,2:T(1,128)S(1)} %copy.199, s32[]{:T(128)S(6)} %copy.221, s32[]{:T(128)} %constant.54.clone.1..sunk, s32[]{:T(128)} %constant.54.clone.1..sunk, s32[]{:T(128)} %constant.54.clone.1..sunk) | dynamic-update-slice | bytes 3145732 | tf_op jit(solution)/shard_map/while/body/jit(dynamic_update_index_in_dim)/dynamic_update_slice | solution.py:207
  708.7 35.7 %fusion.212 = f32[1,1024,6,64]{1,3,2,0:T(8,128)} fusion(f32[6,1024,1024]{1,2,0:T(8,128)} %fusion.209, f32[6,1024,1024]{1,2,0:T(8,128)} %fusion.210, f32[6,1024]{1,0:T(8,128)S(1)} %dynamic-slice_bitcast_fusion.2, pred[1024,1024]{0,1:T(8,128)(4,1)S(1)} %broadcast_compare_fusion.5, bf16[2,1024,6,64]{1,3,2,0:T(8,128)(2,1)} %get-tuple-element.508, ...), kind=kOutput, calls=%fused_computation.45.clone.1 | convolution fusion | flops 874519552 | bytes 105185280 | tf_op jit(solution)/shard_map/while/body/eval_jaxpr/hqk,qhd->khd/dot_general | solution.py:202
  744.4 34.3 %fusion.211 = f32[1,1024,6,64]{1,3,2,0:T(8,128)S(1)} fusion(f32[6,1024,1024]{1,2,0:T(8,128)} %fusion.209, f32[6,1024,1024]{1,2,0:T(8,128)} %fusion.210, f32[6,1024]{1,0:T(8,128)S(1)} %dynamic-slice_bitcast_fusion.2, pred[1024,1024]{0,1:T(8,128)(4,1)S(1)} %broadcast_compare_fusion.5, bf16[2,1024,6,64]{1,3,2,0:T(8,128)(2,1)} %get-tuple-element.506, ...), kind=kOutput, calls=%fused_computation.44.clone.1 | convolution fusion | flops 874519552 | bytes 105185280 | tf_op jit(solution)/shard_map/while/body/eval_jaxpr/hqk,khd->qhd/dot_general | solution.py:199
  783.4 27.5 %dynamic_update_slice.30 = f32[2,1024,6,64]{1,0,3,2:T(2,128)} dynamic-update-slice(f32[2,1024,6,64]{1,0,3,2:T(2,128)} %get-tuple-element.492, f32[1,1024,6,64]{1,0,3,2:T(1,128)S(1)} %copy.200, s32[]{:T(128)S(6)} %copy.221, s32[]{:T(128)} %constant.54.clone.1..sunk, s32[]{:T(128)} %constant.54.clone.1..sunk, s32[]{:T(128)} %constant.54.clone.1..sunk) | dynamic-update-slice | bytes 3145732 | tf_op jit(solution)/shard_map/while/body/jit(dynamic_update_index_in_dim)/dynamic_update_slice | solution.py:207
  810.9 27.5 %dynamic_update_slice.29 = f32[2,1024,6,64]{1,0,3,2:T(2,128)} dynamic-update-slice(f32[2,1024,6,64]{1,0,3,2:T(2,128)} %get-tuple-element.491, f32[1,1024,6,64]{1,0,3,2:T(1,128)S(1)} %copy.199, s32[]{:T(128)S(6)} %copy.221, s32[]{:T(128)} %constant.54.clone.1..sunk, s32[]{:T(128)} %constant.54.clone.1..sunk, s32[]{:T(128)} %constant.54.clone.1..sunk) | dynamic-update-slice | bytes 3145732 | tf_op jit(solution)/shard_map/while/body/jit(dynamic_update_index_in_dim)/dynamic_update_slice | solution.py:207
  989.1 63.4 %reduce-scatter.8.cloned.1.call-done = f32[384,48]{0,1:T(8,128)} async-done(((f32[384,768]{0,1:T(8,128)}), f32[384,48]{0,1:T(8,128)}) %reduce-scatter.8.cloned.1.call-update) | async-done | bytes 73744 | tf_op jit(solution)/shard_map/reduce_scatter | solution.py:231
  1054.1 140.3 %reduce-scatter.10.cloned.1.call-done = f32[48,1536]{1,0:T(8,128)} async-done(((f32[768,1536]{1,0:T(8,128)}), f32[48,1536]{1,0:T(8,128)}) %reduce-scatter.10.cloned.1.call-update) | async-done | bytes 294928 | tf_op jit(solution)/shard_map/reduce_scatter | solution.py:232
  1196.0 141.0 %reduce-scatter.12.cloned.1.call-done = f32[1536,48]{0,1:T(8,128)} async-done(((f32[1536,768]{0,1:T(8,128)}), f32[1536,48]{0,1:T(8,128)}) %reduce-scatter.12.cloned.1.call-update) | async-done | bytes 294928 | tf_op jit(solution)/shard_map/reduce_scatter | solution.py:233
  1338.6 183.0 %all-reduce.11.cloned.1.call-done = f32[3,768,384]{2,0,1:T(4,128)} async-done(((f32[3,768,384]{2,0,1:T(4,128)}), f32[3,768,384]{2,0,1:T(4,128)}) %all-reduce.11.cloned.1.call-update) | async-done | bytes 3538960
  1527.1 120.3 %reduce-scatter.16.cloned.1.call-done = f32[48,8]{1,0:T(8,128)} async-done(((f32[768,8]{1,0:T(8,128)}), f32[48,8]{1,0:T(8,128)}) %reduce-scatter.16.cloned.1.call-update) | async-done | bytes 1552
  1648.8 130.9 %reduce-scatter.14.cloned.1.call-done = f32[128,288]{0,1:T(8,128)} async-done(((f32[128,4608]{0,1:T(8,128)}), f32[128,288]{0,1:T(8,128)}) %reduce-scatter.14.cloned.1.call-update) | async-done | bytes 147472 | tf_op jit(solution)/shard_map/reduce_scatter | solution.py:228
  1792.7 40.0 %psum.39 = f32[]{:T(128)} all-reduce(f32[]{:T(128)S(6)} %add.261), channel_id=1, replica_groups=mesh['dp'=16,'mp'=2] {'dp','mp'}, use_global_device_ids=true, to_apply=%region_34.35 | all-reduce | flops 1 | bytes 8 | tf_op jit(solution)/shard_map/psum | solution.py:250
  (275 shorter events, 506.1 us)
Async XLA Ops:
  7.2 96.6 %all-gather.6.cloned.1.call-start = ((), (), s32[]{:S(2)}) async-start(), calls=%async_computation.5 | async-start | bytes 1253376 | tf_op jit(solution)/shard_map/all_gather | solution.py:100
  8.8 124.7 %all-gather.8.cloned.1.call-start = ((), (), s32[]{:S(2)}) async-start(), calls=%async_computation.6 | async-start | bytes 1880064 | tf_op jit(solution)/shard_map/all_gather | solution.py:102
  10.5 273.7 %all-reduce.7.cloned.1.call-start = ((), (), s32[]{:S(2)}) async-start(), calls=%async_computation.7 | async-start | bytes 12582912 | tf_op jit(solution)/shard_map/psum | solution.py:155
  13.6 106.6 %copy-start.23 = (f32[2048]{0:T(1024)}, f32[2048]{0:T(1024)S(1)}, u32[]{:S(2)}) copy-start(f32[2048]{0:T(1024)S(1)} %broadcast_multiply_fusion.1) | copy-start | bytes 24580
  60.1 60.1 %copy-start.34 = (f32[768]{0:T(1024)}, f32[768]{0:T(1024)S(1)}, u32[]{:S(2)}) copy-start(f32[768]{0:T(1024)S(1)} %get-tuple-element.254) | copy-start | bytes 9220
  60.2 60.1 %copy-start.31 = (f32[2048]{0:T(1024)}, f32[2048]{0:T(1024)S(1)}, u32[]{:S(2)}) copy-start(f32[2048]{0:T(1024)S(1)} %fusion.130) | copy-start | bytes 24580
  60.7 100.9 %copy-start.17 = (f32[1024,32]{0,1:T(8,128)}, f32[1024,32]{0,1:T(8,128)S(1)}, u32[]{:S(2)}) copy-start(f32[1024,32]{0,1:T(8,128)S(1)} %get-tuple-element.336) | copy-start | bytes 393220
  60.7 100.9 %copy-start.19 = (f32[1024,32]{0,1:T(8,128)}, f32[1024,32]{0,1:T(8,128)S(1)}, u32[]{:S(2)}) copy-start(f32[1024,32]{0,1:T(8,128)S(1)} %get-tuple-element.337) | copy-start | bytes 393220
  253.2 98.1 %all-gather.10.cloned.1.call-start = ((), (), s32[]{:S(2)}) async-start(), calls=%async_computation.8 | async-start | bytes 2506752 | tf_op jit(solution)/shard_map/all_gather | solution.py:104
  254.0 162.1 %all-gather.12.cloned.1.call-start = ((), (), s32[]{:S(2)}) async-start(), calls=%async_computation.9 | async-start | bytes 2506752 | tf_op jit(solution)/shard_map/all_gather | solution.py:105
  255.9 216.8 %all-reduce.9.cloned.1.call-start = ((), (), s32[]{:S(2)}) async-start(), calls=%async_computation.10 | async-start | bytes 12582912 | tf_op jit(solution)/shard_map/psum | solution.py:172
  289.7 191.3 %copy-start.25 = (f32[2048]{0:T(1024)}, f32[2048]{0:T(1024)S(1)}, u32[]{:S(2)}) copy-start(f32[2048]{0:T(1024)S(1)} %broadcast_multiply_fusion) | copy-start | bytes 24580
  290.6 190.4 %copy-start.29 = (f32[2048]{0:T(1024)}, f32[2048]{0:T(1024)S(1)}, u32[]{:S(2)}) copy-start(f32[2048]{0:T(1024)S(1)} %fusion.131) | copy-start | bytes 24580
  299.2 116.8 %copy-start.7 = (bf16[2048,768]{1,0:T(8,128)(2,1)S(1)}, bf16[2048,768]{1,0:T(8,128)(2,1)}, u32[]{:S(2)}) copy-start(bf16[2048,768]{1,0:T(8,128)(2,1)} %param.30) | copy-start | bytes 9437188
  441.6 480.6 %all-reduce.13.cloned.1.call-start = ((), (), s32[]{:S(2)}) async-start(), calls=%async_computation.17 | async-start | bytes 25165824 | tf_op jit(solution)/shard_map/psum | solution.py:162
  871.4 181.2 %reduce-scatter.8.cloned.1.call-start = ((), (), s32[]{:S(2)}) async-start(), calls=%async_computation.11 | async-start | bytes 1253376 | tf_op jit(solution)/shard_map/reduce_scatter | solution.py:231
  877.5 316.8 %reduce-scatter.10.cloned.1.call-start = ((), (), s32[]{:S(2)}) async-start(), calls=%async_computation.12 | async-start | bytes 5013504 | tf_op jit(solution)/shard_map/reduce_scatter | solution.py:232
  888.5 448.5 %reduce-scatter.12.cloned.1.call-start = ((), (), s32[]{:S(2)}) async-start(), calls=%async_computation.13 | async-start | bytes 5013504 | tf_op jit(solution)/shard_map/reduce_scatter | solution.py:233
  900.5 621.1 %all-reduce.11.cloned.1.call-start = ((), (), s32[]{:S(2)}) async-start(), calls=%async_computation.16 | async-start | bytes 9437184
  913.3 734.1 %reduce-scatter.16.cloned.1.call-start = ((), (), s32[]{:S(2)}) async-start(), calls=%async_computation.15 | async-start | bytes 417792
  974.2 808.4 %copy-start.4 = (bf16[2048,768]{1,0:T(8,128)(2,1)S(1)}, bf16[2048,768]{1,0:T(8,128)(2,1)}, u32[]{:S(2)}) copy-start(bf16[2048,768]{1,0:T(8,128)(2,1)} %param.27) | copy-start | bytes 9437188
  974.2 805.6 %reduce-scatter.14.cloned.1.call-start = ((), (), s32[]{:S(2)}) async-start(), calls=%async_computation.14 | async-start | bytes 2506752 | tf_op jit(solution)/shard_map/reduce_scatter | solution.py:228
  1782.6 54.4 %copy-start.28 = (f32[384,48]{0,1:T(8,128)S(1)}, f32[384,48]{0,1:T(8,128)}, u32[]{:S(2)}) copy-start(f32[384,48]{0,1:T(8,128)} %param.41) | copy-start | bytes 221188
  1782.6 58.0 %copy-start.22 = (f32[48,1536]{1,0:T(8,128)S(1)}, f32[48,1536]{1,0:T(8,128)}, u32[]{:S(2)}) copy-start(f32[48,1536]{1,0:T(8,128)} %param.44) | copy-start | bytes 884740
  (43 other events, 435.6 us)
Sparse Core Ops, SparseCore 0:
  11.4 59.7 all-gather.5
  74.5 58.9 all-gather.7
  253.3 30.7 all-reduce.6
  287.8 63.4 all-gather.9
  354.9 61.0 all-gather.11
  441.7 30.8 all-reduce.8
  871.5 50.6 all-reduce.12
  927.0 125.5 reduce-scatter.7
  1057.8 136.5 reduce-scatter.9
  1200.2 136.7 reduce-scatter.11
  1342.7 178.8 all-reduce.10
  1526.8 120.5 reduce-scatter.15
  1652.3 127.3 reduce-scatter.13
where the time goes:
time: 1860 us; the launch traced here: 1850 us
  waiting for transfers between devices  947 us (51%)
  matrix products  399 us (21%)
  other arithmetic  180 us (10%)
  local copies, waits for them, and re-layouts  178 us (10%)
  blocking collectives  126 us (7%)
  between operations  22.2 us (1%)
    unnamed x15, waiting for transfers between devices  303 us
    reduce_scatter x1, waiting for transfers between devices, per_device(): lax.psum_scatter(grad_down, 'dp', scatter_dimension=1, tiled=True)  141 us
    reduce_scatter x1, waiting for transfers between devices, per_device(): lax.psum_scatter(grad_up, 'dp', scatter_dimension=0, tiled=True)  140 us
    reduce_scatter x1, waiting for transfers between devices, per_device(): lax.psum_scatter(grad_ada, 'dp', scatter_dimension=1, tiled=True)  131 us
    dynamic_update_slice x8, local copies, waits for them, and re-layouts, per_device(): lax.map(attend_back, (queries, keys, values, segments, logsums, grad_atte...  119 us
    dot_general x2, matrix products, attend_back(): jnp.einsum('hqk,qhd->khd', grad_scores, query_block, preferred_element_ty...  71.3 us
    dot_general x2, matrix products, attend_back(): jnp.einsum('hqk,khd->qhd', grad_scores, key_block, preferred_element_type...  68.8 us
    reduce_scatter x1, waiting for transfers between devices, per_device(): lax.psum_scatter(grad_out, 'dp', scatter_dimension=1, tiled=True)  63.4 us
  transfers between devices with their start and end apart: 13, of which 12 were waited for; matrix products, arithmetic and copies ran while one was open for 10% of the time, Pallas kernels for 0%

commit v1 on v0

--- a/solution.py
+++ b/solution.py
@@ -247,7 +247,7 @@
         + jnp.sum(down_mean * down_mean)
         + shared_part * (jnp.sum(ada_mean * ada_mean) + jnp.sum(norm_mean * norm_mean))
     )
-    total_sq = lax.psum(local_sq, ("dp", "mp"))
+    total_sq = jnp.sum(lax.all_gather(local_sq, ("dp", "mp")), axis=0)
     grad_norm = jnp.sqrt(total_sq)
     clip_factor = jnp.minimum(1.0, clip_limit / (grad_norm + 1e-06))
     step_count = step[0].astype(jnp.float32)

time: 1860 us -> 1870 us (level)
    unnamed x0 -> x1, blocking collectives: none -> 40.3 us
    psum x1 -> x0, blocking collectives: 40 us -> none  [per_device(): total_sq = lax.psum(local_sq, ('dp', 'mp'))]
where the time goes in v1:
time: 1870 us; the launch traced here: 1860 us
  waiting for transfers between devices  947 us (51%)
  matrix products  399 us (21%)
  other arithmetic  181 us (10%)
  local copies, waits for them, and re-layouts  180 us (10%)
  blocking collectives  126 us (7%)
  between operations  22.2 us (1%)
    unnamed x15, waiting for transfers between devices  304 us
    reduce_scatter x1, waiting for transfers between devices, per_device(): lax.psum_scatter(grad_down, 'dp', scatter_dimension=1, tiled=True)  141 us
    reduce_scatter x1, waiting for transfers between devices, per_device(): lax.psum_scatter(grad_up, 'dp', scatter_dimension=0, tiled=True)  140 us
    reduce_scatter x1, waiting for transfers between devices, per_device(): lax.psum_scatter(grad_ada, 'dp', scatter_dimension=1, tiled=True)  131 us
    dynamic_update_slice x8, local copies, waits for them, and re-layouts, per_device(): lax.map(attend_back, (queries, keys, values, segments, logsums, grad_atte...  120 us
    dot_general x2, matrix products, attend_back(): jnp.einsum('hqk,qhd->khd', grad_scores, query_block, preferred_element_ty...  71.4 us
    dot_general x2, matrix products, attend_back(): jnp.einsum('hqk,khd->qhd', grad_scores, key_block, preferred_element_type...  68.8 us
    reduce_scatter x1, waiting for transfers between devices, per_device(): lax.psum_scatter(grad_out, 'dp', scatter_dimension=1, tiled=True)  63.2 us
  transfers between devices with their start and end apart: 13, of which 12 were waited for; matrix products, arithmetic and copies ran while one was open for 10% of the time, Pallas kernels for 0%

profile of v1, /device:TPU:0, one launch (start us, length us, event | category | flops | bytes accessed | tf_op | source)
XLA Modules:
  0.0 1856.1 jit_solution(2001908157346540740)
XLA Ops:
  16.6 42.8 %all-gather = bf16[16,48,8]{1,2,0:T(8,128)(2,1)S(1)} all-gather(bf16[1,48,8]{1,2,0:T(8,128)(2,1)S(1)} %convert_bitcast_fusion), channel_id=1, replica_groups=mesh['dp'=16,'mp'=2] {'dp'}, dimensions={0}, use_global_device_ids=true | all-gather | bytes 13056 | tf_op jit(solution)/shard_map/all_gather | solution.py:101
  60.7 43.1 %all_gather.27 = bf16[384,768]{0,1:T(8,128)(2,1)} all-gather(bf16[384,48]{0,1:T(8,128)(2,1)S(1)} %convert_element_type.96), channel_id=1, replica_groups=mesh['dp'=16,'mp'=2] {'dp'}, dimensions={1}, use_global_device_ids=true | all-gather | bytes 626688 | tf_op jit(solution)/shard_map/all_gather | solution.py:103
  103.8 16.3 convolution_add_fusion
  174.9 70.6 %while.26 = (s32[]{:T(128)}, bf16[2,1024,6,64]{1,3,2,0:T(8,128)(2,1)S(1)}, f32[2,6,1024,1]{2,1,3,0:T(8,128)S(1)}, bf16[2,1024,6,64]{1,3,2,0:T(8,128)(2,1)}, s32[...) while((s32[]{:T(128)}, ...), condition=%wide.region_5.6_spmd, body=%wide.region_2.5_spmd.sunk | while | flops 1681254400 | bytes 83089512 | solution.py:152
  255.9 28.3 %all-reduce.8.cloned.1.call-done = f32[2048,768]{1,0:T(8,128)} async-done(((f32[2048,768]{1,0:T(8,128)}), f32[2048,768]{1,0:T(8,128)}) %all-reduce.8.cloned.1.call-update) | async-done | bytes 6291472 | tf_op jit(solution)/shard_map/psum | solution.py:155
  299.5 51.9 %all-gather.10.cloned.1.call-done = bf16[768,1536]{1,0:T(8,128)(2,1)} async-done(((bf16[48,1536]{1,0:T(8,128)(2,1)}), bf16[768,1536]{1,0:T(8,128)(2,1)}) %all-gather.10.cloned.1.call-update) | async-done | bytes 2359312 | tf_op jit(solution)/shard_map/all_gather | solution.py:104
  364.4 51.7 %all-gather.12.cloned.1.call-done = bf16[1536,768]{0,1:T(8,128)(2,1)} async-done(((bf16[1536,48]{0,1:T(8,128)(2,1)}), bf16[1536,768]{0,1:T(8,128)(2,1)}) %all-gather.12.cloned.1.call-update) | async-done | bytes 2359312 | tf_op jit(solution)/shard_map/all_gather | solution.py:105
  452.0 20.8 %all-reduce.10.cloned.1.call-done = f32[2048,768]{1,0:T(8,128)} async-done(((f32[2048,768]{1,0:T(8,128)}), f32[2048,768]{1,0:T(8,128)}) %all-reduce.10.cloned.1.call-update) | async-done | bytes 6291472 | tf_op jit(solution)/shard_map/psum | solution.py:172
  500.2 339.3 %while.27 = (s32[]{:T(128)}, f32[2,1024,6,64]{1,0,3,2:T(2,128)}, f32[2,1024,6,64]{1,0,3,2:T(2,128)}, bf16[2,1024,6,64]{1,3,2,0:T(8,128)(2,1)}, bf16[2,1024,6,64]...) while((s32[]{:T(128)}, f32[2,1024,6,64]{1,0,3,2:T(2,128)}, ...), condition=%wide.region_15.16_spmd, body=%wide.region_13.15_spmd.sunk | while | flops 4191172608 | bytes 306142336 | solution.py:207
  539.8 35.6 %fusion.212 = f32[1,1024,6,64]{1,3,2,0:T(8,128)} fusion(f32[6,1024,1024]{1,2,0:T(8,128)} %fusion.209, f32[6,1024,1024]{1,2,0:T(8,128)} %fusion.210, f32[6,1024]{1,0:T(8,128)S(1)} %dynamic-slice_bitcast_fusion.2, pred[1024,1024]{0,1:T(8,128)(4,1)S(1)} %broadcast_compare_fusion.5, bf16[2,1024,6,64]{1,3,2,0:T(8,128)(2,1)} %get-tuple-element.508, ...), kind=kOutput, calls=%fused_computation.45.clone.1 | convolution fusion | flops 874519552 | bytes 105185280 | tf_op jit(solution)/shard_map/while/body/eval_jaxpr/hqk,qhd->khd/dot_general | solution.py:202
  575.4 34.5 %fusion.211 = f32[1,1024,6,64]{1,3,2,0:T(8,128)S(1)} fusion(f32[6,1024,1024]{1,2,0:T(8,128)} %fusion.209, f32[6,1024,1024]{1,2,0:T(8,128)} %fusion.210, f32[6,1024]{1,0:T(8,128)S(1)} %dynamic-slice_bitcast_fusion.2, pred[1024,1024]{0,1:T(8,128)(4,1)S(1)} %broadcast_compare_fusion.5, bf16[2,1024,6,64]{1,3,2,0:T(8,128)(2,1)} %get-tuple-element.506, ...), kind=kOutput, calls=%fused_computation.44.clone.1 | convolution fusion | flops 874519552 | bytes 105185280 | tf_op jit(solution)/shard_map/while/body/eval_jaxpr/hqk,khd->qhd/dot_general | solution.py:199
  614.6 27.6 %dynamic_update_slice.30 = f32[2,1024,6,64]{1,0,3,2:T(2,128)} dynamic-update-slice(f32[2,1024,6,64]{1,0,3,2:T(2,128)} %get-tuple-element.492, f32[1,1024,6,64]{1,0,3,2:T(1,128)S(1)} %copy.201, s32[]{:T(128)S(6)} %copy.222, s32[]{:T(128)} %constant.54.clone.1..sunk, s32[]{:T(128)} %constant.54.clone.1..sunk, s32[]{:T(128)} %constant.54.clone.1..sunk) | dynamic-update-slice | bytes 3145732 | tf_op jit(solution)/shard_map/while/body/jit(dynamic_update_index_in_dim)/dynamic_update_slice | solution.py:207
  642.2 27.6 %dynamic_update_slice.29 = f32[2,1024,6,64]{1,0,3,2:T(2,128)} dynamic-update-slice(f32[2,1024,6,64]{1,0,3,2:T(2,128)} %get-tuple-element.491, f32[1,1024,6,64]{1,0,3,2:T(1,128)S(1)} %copy.200, s32[]{:T(128)S(6)} %copy.222, s32[]{:T(128)} %constant.54.clone.1..sunk, s32[]{:T(128)} %constant.54.clone.1..sunk, s32[]{:T(128)} %constant.54.clone.1..sunk) | dynamic-update-slice | bytes 3145732 | tf_op jit(solution)/shard_map/while/body/jit(dynamic_update_index_in_dim)/dynamic_update_slice | solution.py:207
  709.2 35.7 %fusion.212 = f32[1,1024,6,64]{1,3,2,0:T(8,128)} fusion(f32[6,1024,1024]{1,2,0:T(8,128)} %fusion.209, f32[6,1024,1024]{1,2,0:T(8,128)} %fusion.210, f32[6,1024]{1,0:T(8,128)S(1)} %dynamic-slice_bitcast_fusion.2, pred[1024,1024]{0,1:T(8,128)(4,1)S(1)} %broadcast_compare_fusion.5, bf16[2,1024,6,64]{1,3,2,0:T(8,128)(2,1)} %get-tuple-element.508, ...), kind=kOutput, calls=%fused_computation.45.clone.1 | convolution fusion | flops 874519552 | bytes 105185280 | tf_op jit(solution)/shard_map/while/body/eval_jaxpr/hqk,qhd->khd/dot_general | solution.py:202
  744.9 34.4 %fusion.211 = f32[1,1024,6,64]{1,3,2,0:T(8,128)S(1)} fusion(f32[6,1024,1024]{1,2,0:T(8,128)} %fusion.209, f32[6,1024,1024]{1,2,0:T(8,128)} %fusion.210, f32[6,1024]{1,0:T(8,128)S(1)} %dynamic-slice_bitcast_fusion.2, pred[1024,1024]{0,1:T(8,128)(4,1)S(1)} %broadcast_compare_fusion.5, bf16[2,1024,6,64]{1,3,2,0:T(8,128)(2,1)} %get-tuple-element.506, ...), kind=kOutput, calls=%fused_computation.44.clone.1 | convolution fusion | flops 874519552 | bytes 105185280 | tf_op jit(solution)/shard_map/while/body/eval_jaxpr/hqk,khd->qhd/dot_general | solution.py:199
  784.0 27.6 %dynamic_update_slice.30 = f32[2,1024,6,64]{1,0,3,2:T(2,128)} dynamic-update-slice(f32[2,1024,6,64]{1,0,3,2:T(2,128)} %get-tuple-element.492, f32[1,1024,6,64]{1,0,3,2:T(1,128)S(1)} %copy.201, s32[]{:T(128)S(6)} %copy.222, s32[]{:T(128)} %constant.54.clone.1..sunk, s32[]{:T(128)} %constant.54.clone.1..sunk, s32[]{:T(128)} %constant.54.clone.1..sunk) | dynamic-update-slice | bytes 3145732 | tf_op jit(solution)/shard_map/while/body/jit(dynamic_update_index_in_dim)/dynamic_update_slice | solution.py:207
  811.6 27.6 %dynamic_update_slice.29 = f32[2,1024,6,64]{1,0,3,2:T(2,128)} dynamic-update-slice(f32[2,1024,6,64]{1,0,3,2:T(2,128)} %get-tuple-element.491, f32[1,1024,6,64]{1,0,3,2:T(1,128)S(1)} %copy.200, s32[]{:T(128)S(6)} %copy.222, s32[]{:T(128)} %constant.54.clone.1..sunk, s32[]{:T(128)} %constant.54.clone.1..sunk, s32[]{:T(128)} %constant.54.clone.1..sunk) | dynamic-update-slice | bytes 3145732 | tf_op jit(solution)/shard_map/while/body/jit(dynamic_update_index_in_dim)/dynamic_update_slice | solution.py:207
  990.2 63.2 %reduce-scatter.8.cloned.1.call-done = f32[384,48]{0,1:T(8,128)} async-done(((f32[384,768]{0,1:T(8,128)}), f32[384,48]{0,1:T(8,128)}) %reduce-scatter.8.cloned.1.call-update) | async-done | bytes 73744 | tf_op jit(solution)/shard_map/reduce_scatter | solution.py:231
  1054.9 140.2 %reduce-scatter.10.cloned.1.call-done = f32[48,1536]{1,0:T(8,128)} async-done(((f32[768,1536]{1,0:T(8,128)}), f32[48,1536]{1,0:T(8,128)}) %reduce-scatter.10.cloned.1.call-update) | async-done | bytes 294928 | tf_op jit(solution)/shard_map/reduce_scatter | solution.py:232
  1196.8 140.7 %reduce-scatter.12.cloned.1.call-done = f32[1536,48]{0,1:T(8,128)} async-done(((f32[1536,768]{0,1:T(8,128)}), f32[1536,48]{0,1:T(8,128)}) %reduce-scatter.12.cloned.1.call-update) | async-done | bytes 294928 | tf_op jit(solution)/shard_map/reduce_scatter | solution.py:233
  1339.1 183.0 %all-reduce.12.cloned.1.call-done = f32[3,768,384]{2,0,1:T(4,128)} async-done(((f32[3,768,384]{2,0,1:T(4,128)}), f32[3,768,384]{2,0,1:T(4,128)}) %all-reduce.12.cloned.1.call-update) | async-done | bytes 3538960
  1527.7 120.3 %reduce-scatter.16.cloned.1.call-done = f32[48,8]{1,0:T(8,128)} async-done(((f32[768,8]{1,0:T(8,128)}), f32[48,8]{1,0:T(8,128)}) %reduce-scatter.16.cloned.1.call-update) | async-done | bytes 1552
  1649.4 130.9 %reduce-scatter.14.cloned.1.call-done = f32[128,288]{0,1:T(8,128)} async-done(((f32[128,4608]{0,1:T(8,128)}), f32[128,288]{0,1:T(8,128)}) %reduce-scatter.14.cloned.1.call-update) | async-done | bytes 147472 | tf_op jit(solution)/shard_map/reduce_scatter | solution.py:228
  1795.0 40.3 %all-reduce = f32[32]{0:T(128)S(1)} all-reduce(f32[32]{0:T(128)} %dynamic-update-slice), channel_id=1, replica_groups=mesh['dp'=16,'mp'=2] {'dp','mp'}, use_global_device_ids=true, to_apply=%add | all-reduce | flops 32 | bytes 256
  (278 shorter events, 509.2 us)
Async XLA Ops:
  7.2 96.6 %all-gather.6.cloned.1.call-start = ((), (), s32[]{:S(2)}) async-start(), calls=%async_computation.5 | async-start | bytes 1253376 | tf_op jit(solution)/shard_map/all_gather | solution.py:100
  8.8 124.7 %all-gather.8.cloned.1.call-start = ((), (), s32[]{:S(2)}) async-start(), calls=%async_computation.6 | async-start | bytes 1880064 | tf_op jit(solution)/shard_map/all_gather | solution.py:102
  10.5 273.7 %all-reduce.8.cloned.1.call-start = ((), (), s32[]{:S(2)}) async-start(), calls=%async_computation.7 | async-start | bytes 12582912 | tf_op jit(solution)/shard_map/psum | solution.py:155
  13.6 106.5 %copy-start.23 = (f32[2048]{0:T(1024)}, f32[2048]{0:T(1024)S(1)}, u32[]{:S(2)}) copy-start(f32[2048]{0:T(1024)S(1)} %broadcast_multiply_fusion.1) | copy-start | bytes 24580
  60.1 60.0 %copy-start.34 = (f32[768]{0:T(1024)}, f32[768]{0:T(1024)S(1)}, u32[]{:S(2)}) copy-start(f32[768]{0:T(1024)S(1)} %get-tuple-element.254) | copy-start | bytes 9220
  60.2 60.0 %copy-start.31 = (f32[2048]{0:T(1024)}, f32[2048]{0:T(1024)S(1)}, u32[]{:S(2)}) copy-start(f32[2048]{0:T(1024)S(1)} %fusion.130) | copy-start | bytes 24580
  60.7 100.9 %copy-start.17 = (f32[1024,32]{0,1:T(8,128)}, f32[1024,32]{0,1:T(8,128)S(1)}, u32[]{:S(2)}) copy-start(f32[1024,32]{0,1:T(8,128)S(1)} %get-tuple-element.336) | copy-start | bytes 393220
  60.7 100.9 %copy-start.19 = (f32[1024,32]{0,1:T(8,128)}, f32[1024,32]{0,1:T(8,128)S(1)}, u32[]{:S(2)}) copy-start(f32[1024,32]{0,1:T(8,128)S(1)} %get-tuple-element.337) | copy-start | bytes 393220
  253.3 98.1 %all-gather.10.cloned.1.call-start = ((), (), s32[]{:S(2)}) async-start(), calls=%async_computation.8 | async-start | bytes 2506752 | tf_op jit(solution)/shard_map/all_gather | solution.py:104
  254.0 162.0 %all-gather.12.cloned.1.call-start = ((), (), s32[]{:S(2)}) async-start(), calls=%async_computation.9 | async-start | bytes 2506752 | tf_op jit(solution)/shard_map/all_gather | solution.py:105
  255.9 216.9 %all-reduce.10.cloned.1.call-start = ((), (), s32[]{:S(2)}) async-start(), calls=%async_computation.10 | async-start | bytes 12582912 | tf_op jit(solution)/shard_map/psum | solution.py:172
  289.9 191.2 %copy-start.25 = (f32[2048]{0:T(1024)}, f32[2048]{0:T(1024)S(1)}, u32[]{:S(2)}) copy-start(f32[2048]{0:T(1024)S(1)} %broadcast_multiply_fusion) | copy-start | bytes 24580
  290.8 190.3 %copy-start.29 = (f32[2048]{0:T(1024)}, f32[2048]{0:T(1024)S(1)}, u32[]{:S(2)}) copy-start(f32[2048]{0:T(1024)S(1)} %fusion.131) | copy-start | bytes 24580
  299.5 116.6 %copy-start.7 = (bf16[2048,768]{1,0:T(8,128)(2,1)S(1)}, bf16[2048,768]{1,0:T(8,128)(2,1)}, u32[]{:S(2)}) copy-start(bf16[2048,768]{1,0:T(8,128)(2,1)} %param.30) | copy-start | bytes 9437188
  441.8 481.3 %all-reduce.14.cloned.1.call-start = ((), (), s32[]{:S(2)}) async-start(), calls=%async_computation.17 | async-start | bytes 25165824 | tf_op jit(solution)/shard_map/psum | solution.py:162
  872.2 181.2 %reduce-scatter.8.cloned.1.call-start = ((), (), s32[]{:S(2)}) async-start(), calls=%async_computation.11 | async-start | bytes 1253376 | tf_op jit(solution)/shard_map/reduce_scatter | solution.py:231
  878.4 316.8 %reduce-scatter.10.cloned.1.call-start = ((), (), s32[]{:S(2)}) async-start(), calls=%async_computation.12 | async-start | bytes 5013504 | tf_op jit(solution)/shard_map/reduce_scatter | solution.py:232
  889.3 448.2 %reduce-scatter.12.cloned.1.call-start = ((), (), s32[]{:S(2)}) async-start(), calls=%async_computation.13 | async-start | bytes 5013504 | tf_op jit(solution)/shard_map/reduce_scatter | solution.py:233
  901.3 620.8 %all-reduce.12.cloned.1.call-start = ((), (), s32[]{:S(2)}) async-start(), calls=%async_computation.16 | async-start | bytes 9437184
  914.1 733.9 %reduce-scatter.16.cloned.1.call-start = ((), (), s32[]{:S(2)}) async-start(), calls=%async_computation.15 | async-start | bytes 417792
  975.3 809.7 %copy-start.4 = (bf16[2048,768]{1,0:T(8,128)(2,1)S(1)}, bf16[2048,768]{1,0:T(8,128)(2,1)}, u32[]{:S(2)}) copy-start(bf16[2048,768]{1,0:T(8,128)(2,1)} %param.27) | copy-start | bytes 9437188
  975.3 805.1 %reduce-scatter.14.cloned.1.call-start = ((), (), s32[]{:S(2)}) async-start(), calls=%async_computation.14 | async-start | bytes 2506752 | tf_op jit(solution)/shard_map/reduce_scatter | solution.py:228
  1785.0 55.2 %copy-start.28 = (f32[384,48]{0,1:T(8,128)S(1)}, f32[384,48]{0,1:T(8,128)}, u32[]{:S(2)}) copy-start(f32[384,48]{0,1:T(8,128)} %param.41) | copy-start | bytes 221188
  1785.0 58.8 %copy-start.22 = (f32[48,1536]{1,0:T(8,128)S(1)}, f32[48,1536]{1,0:T(8,128)}, u32[]{:S(2)}) copy-start(f32[48,1536]{1,0:T(8,128)} %param.44) | copy-start | bytes 884740
  (43 other events, 435.8 us)
Sparse Core Ops, SparseCore 0:
  11.4 59.7 all-gather.5
  74.5 58.9 all-gather.7
  253.4 30.7 all-reduce.7
  287.8 63.4 all-gather.9
  354.9 61.0 all-gather.11
  441.9 30.8 all-reduce.9
  872.3 50.6 all-reduce.13
  927.8 125.5 reduce-scatter.7
  1058.6 136.4 reduce-scatter.9
  1201.0 136.4 reduce-scatter.11
  1343.2 178.8 all-reduce.11
  1527.4 120.5 reduce-scatter.15
  1652.9 127.3 reduce-scatter.13
